TPU v7x, 512 devices: a whole 4x4x16 slice. The times are simulated.
512 devices in a mesh: patch: 64 (over x, z_hi, y, core), uly: 8 (over z_lo).
Axes of the slice: x: 4, y: 4, z: 16 (z_hi: 2, z_lo: 8; z = z_hi * 8 + z_lo), core: 2. Of those that a mesh axis runs over, the one named last changes fastest.
Arguments:
- queries: bfloat16 [8192, 3072], P(('patch', 'uly')), may hold values from -512 to 512
- keys_new: bfloat16 [8192, 3072], P(('patch', 'uly')), may hold values from -6 to 6
- values_new: bfloat16 [8192, 3072], P(('patch', 'uly')), may hold values from -6 to 6
- keys_old: bfloat16 [8192, 3072], P(('patch', 'uly')), may hold values from -8 to 8
- values_old: bfloat16 [8192, 3072], P(('patch', 'uly')), may hold values from -6 to 6
- gate_table: float32 [50, 3072], replicated, may hold values from 0.5 to 2
- step_index: int32 [1], replicated, may hold values from 0 to 49
Outputs:
- attended: bfloat16 [8192, 3072], P(('patch', 'uly'))
All inputs are finite; a program needn't handle non-finite values.
Results may differ from a plain program's by a relative error of at most 0.0045.
Values may be sent and summed in bfloat16 or wider, within the bound.
A program may use at most 64 MiB of HBM per device.

v0:
```python
import jax
import jax.numpy as jnp
from jax import lax
from jax.sharding import PartitionSpec as P

HEADS = 24
HEAD_DIM = 128


def sent_together(arrays, axis, dim, along):
    both = jnp.concatenate(arrays, axis=along)
    result, at, outs = (lax.all_gather(both, axis, axis=dim, tiled=True), 0, [])
    for a in arrays:
        outs.append(lax.slice_in_dim(result, at, at + a.shape[along], axis=along))
        at += a.shape[along]
    return tuple(outs)


def absorb(carry, query_heads, key_piece, value_piece, masked):
    run_max, run_total, accumulated = carry
    score = jnp.einsum(
        "phd,khd->hpk", query_heads, key_piece, preferred_element_type=jnp.float32
    ) * HEAD_DIM ** (-0.5)
    score = jnp.where(masked[None, None, :], jnp.float32(-1e30), score)
    new_max = jnp.maximum(run_max, jnp.max(score, axis=-1))
    shrink = jnp.exp(run_max - new_max)
    expo = jnp.exp(score - new_max[..., None])
    run_total = run_total * shrink + jnp.sum(expo, axis=-1)
    update = jnp.einsum(
        "hpk,khd->phd", expo.astype(jnp.bfloat16), value_piece, preferred_element_type=jnp.float32
    )
    accumulated = accumulated * jnp.transpose(shrink)[..., None] + update
    return (new_max, run_total, accumulated)


def absorb_blocks(carry, query_heads, key_piece, value_piece, masked):
    count = key_piece.shape[0]
    span = 2048
    heads_here = key_piece.shape[1]
    key_blocks = key_piece.reshape(count // span, span, heads_here, HEAD_DIM)
    value_blocks = value_piece.reshape(count // span, span, heads_here, HEAD_DIM)
    mask_blocks = masked.reshape(count // span, span)

    def one_block(state, pieces):
        return (absorb(state, query_heads, pieces[0], pieces[1], pieces[2]), None)

    carry, unused = lax.scan(one_block, carry, (key_blocks, value_blocks, mask_blocks))
    return carry


def body(queries, keys_new, values_new, keys_old, values_old, gate_table, step_index):
    groups = lax.axis_size("uly")
    heads_here = HEADS // groups
    width_here = heads_here * HEAD_DIM
    patch_here = lax.axis_index("patch")
    fresh = (
        lax.all_to_all(queries, "uly", split_axis=1, concat_axis=0, tiled=True),
        lax.all_to_all(keys_new, "uly", split_axis=1, concat_axis=0, tiled=True),
        lax.all_to_all(values_new, "uly", split_axis=1, concat_axis=0, tiled=True),
    )
    query_heads = fresh[0].reshape(-1, heads_here, HEAD_DIM)
    fresh_keys = fresh[1].reshape(-1, heads_here, HEAD_DIM)
    fresh_values = fresh[2].reshape(-1, heads_here, HEAD_DIM)
    patch_rows = query_heads.shape[0]
    score = jnp.einsum(
        "phd,khd->hpk", query_heads, fresh_keys, preferred_element_type=jnp.float32
    ) * HEAD_DIM ** (-0.5)
    run_max = jnp.max(score, axis=-1)
    expo = jnp.exp(score - run_max[..., None])
    run_total = jnp.sum(expo, axis=-1)
    accumulated = jnp.einsum(
        "hpk,khd->phd", expo.astype(jnp.bfloat16), fresh_values, preferred_element_type=jnp.float32
    )
    carry = (run_max, run_total, accumulated)
    stale = (
        lax.all_to_all(keys_old, "uly", split_axis=1, concat_axis=0, tiled=True),
        lax.all_to_all(values_old, "uly", split_axis=1, concat_axis=0, tiled=True),
    )
    stale_keys = stale[0].reshape(-1, heads_here, HEAD_DIM)
    stale_values = stale[1].reshape(-1, heads_here, HEAD_DIM)
    pieces = sent_together((stale_keys, stale_values), "patch", 0, 1)
    count = pieces[0].shape[0]
    masked = jnp.arange(count, dtype=jnp.int32) // patch_rows == patch_here
    carry = absorb_blocks(carry, query_heads, pieces[0], pieces[1], masked)
    run_max, run_total, accumulated = carry
    picker = (jnp.arange(gate_table.shape[0], dtype=jnp.int32) == step_index[0]).astype(jnp.float32)
    gate = jnp.dot(picker, gate_table, precision=lax.Precision.HIGHEST)
    gate_here = lax.dynamic_slice_in_dim(gate, lax.axis_index("uly") * width_here, width_here, 0)
    mixed = (accumulated / jnp.transpose(run_total)[..., None]).reshape(patch_rows, width_here)
    gated = (mixed * gate_here).astype(jnp.bfloat16)
    return lax.all_to_all(gated, "uly", split_axis=0, concat_axis=1, tiled=True)


def solution(mesh):
    in_specs = (
        P(("patch", "uly"), None),
        P(("patch", "uly"), None),
        P(("patch", "uly"), None),
        P(("patch", "uly"), None),
        P(("patch", "uly"), None),
        P(),
        P(),
    )
    out_specs = P(("patch", "uly"), None)
    return jax.shard_map(body, mesh=mesh, in_specs=in_specs, out_specs=out_specs, check_vma=False)
```

profile of v0, /device:TPU:8, one launch (start us, length us, event | category | flops | bytes accessed | tf_op | source)
XLA Modules:
  0.0 314.0 jit_solution(12219189061899668328)
XLA Ops:
  6.5 0.0 copy-start
  6.5 0.0 copy-start.1
  6.5 1.6 copy.86
  8.1 12.5 %all-to-all-start.3 = ((bf16[16,8,384]{2,0,1:T(8,128)(2,1)}), bf16[16,8,384]{2,0,1:T(8,128)(2,1)S(1)}, u32[]{:S(2)}, u32[]{:S(2)}) async-start(bf16[16,8,384]{2,0,1:T(8,128)(2,1)} %bitcast.72), calls=%async_computation.3 | async-start | bytes 196608 | tf_op jit(solution)/shard_map/all_to_all | solution.py:76
  20.7 1.5 copy.85
  22.2 9.7 %all-to-all-done.3 = bf16[16,8,384]{2,0,1:T(8,128)(2,1)S(1)} async-done(((bf16[16,8,384]{2,0,1:T(8,128)(2,1)}), bf16[16,8,384]{2,0,1:T(8,128)(2,1)S(1)}, u32[]{:S(2)}, u32[]{:S(2)}) %all-to-all-start.3) | async-done | bytes 98336 | tf_op jit(solution)/shard_map/all_to_all | solution.py:76
  31.9 3.6 %all-to-all-start.4 = ((bf16[16,8,384]{2,0,1:T(8,128)(2,1)}), bf16[16,8,384]{2,0,1:T(8,128)(2,1)S(1)}, u32[]{:S(2)}, u32[]{:S(2)}) async-start(bf16[16,8,384]{2,0,1:T(8,128)(2,1)} %bitcast.71), calls=%async_computation.4 | async-start | bytes 196608 | tf_op jit(solution)/shard_map/all_to_all | solution.py:77
  35.5 0.0 all-gather.2.cloned.1.call-start
  35.6 11.1 %all-to-all-done.4 = bf16[16,8,384]{2,0,1:T(8,128)(2,1)S(1)} async-done(((bf16[16,8,384]{2,0,1:T(8,128)(2,1)}), bf16[16,8,384]{2,0,1:T(8,128)(2,1)S(1)}, u32[]{:S(2)}, u32[]{:S(2)}) %all-to-all-start.4) | async-done | bytes 98336 | tf_op jit(solution)/shard_map/all_to_all | solution.py:77
  46.7 0.1 pad_maximum_fusion
  46.9 0.7 copy.57
  47.6 0.0 all-gather.2.cloned.1.call-update
  47.6 1.5 copy.89
  49.2 3.5 %all-to-all-start = ((bf16[16,8,384]{2,0,1:T(8,128)(2,1)}), bf16[16,8,384]{2,0,1:T(8,128)(2,1)S(1)}, u32[]{:S(2)}, u32[]{:S(2)}) async-start(bf16[16,8,384]{2,0,1:T(8,128)(2,1)} %bitcast.75), calls=%async_computation | async-start | bytes 196608 | tf_op jit(solution)/shard_map/all_to_all | solution.py:57
  52.6 1.5 copy.88
  54.2 9.6 %all-to-all-done = bf16[16,8,384]{2,0,1:T(8,128)(2,1)S(1)} async-done(((bf16[16,8,384]{2,0,1:T(8,128)(2,1)}), bf16[16,8,384]{2,0,1:T(8,128)(2,1)S(1)}, u32[]{:S(2)}, u32[]{:S(2)}) %all-to-all-start) | async-done | bytes 98336 | tf_op jit(solution)/shard_map/all_to_all | solution.py:57
  63.8 3.4 %all-to-all-start.1 = ((bf16[16,8,384]{2,0,1:T(8,128)(2,1)}), bf16[16,8,384]{2,0,1:T(8,128)(2,1)S(1)}, u32[]{:S(2)}, u32[]{:S(2)}) async-start(bf16[16,8,384]{2,0,1:T(8,128)(2,1)} %bitcast.74), calls=%async_computation.1 | async-start | bytes 196608 | tf_op jit(solution)/shard_map/all_to_all | solution.py:58
  67.2 0.0 copy-done.1
  67.2 0.7 copy.87
  68.5 13.1 %all-to-all-done.1 = bf16[16,8,384]{2,0,1:T(8,128)(2,1)S(1)} async-done(((bf16[16,8,384]{2,0,1:T(8,128)(2,1)}), bf16[16,8,384]{2,0,1:T(8,128)(2,1)S(1)}, u32[]{:S(2)}, u32[]{:S(2)}) %all-to-all-start.1) | async-done | bytes 98336 | tf_op jit(solution)/shard_map/all_to_all | solution.py:58
  81.6 3.4 %all-to-all-start.2 = ((bf16[16,8,384]{2,0,1:T(8,128)(2,1)}), bf16[16,8,384]{2,0,1:T(8,128)(2,1)S(1)}, u32[]{:S(2)}, u32[]{:S(2)}) async-start(bf16[16,8,384]{2,0,1:T(8,128)(2,1)} %bitcast.73), calls=%async_computation.2 | async-start | bytes 196608 | tf_op jit(solution)/shard_map/all_to_all | solution.py:59
  85.0 0.0 copy-done
  85.0 0.3 fusion.33
  85.3 0.1 dynamic_slice.14
  85.4 0.1 fusion.30
  85.6 10.6 %all-to-all-done.2 = bf16[16,8,384]{2,0,1:T(8,128)(2,1)S(1)} async-done(((bf16[16,8,384]{2,0,1:T(8,128)(2,1)}), bf16[16,8,384]{2,0,1:T(8,128)(2,1)S(1)}, u32[]{:S(2)}, u32[]{:S(2)}) %all-to-all-start.2) | async-done | bytes 98336 | tf_op jit(solution)/shard_map/all_to_all | solution.py:59
  96.2 0.2 fusion.39
  96.5 0.2 convolution_bitcast_fusion
  96.7 0.1 copy.58
  96.8 0.1 fusion.24
  96.9 165.4 %all-gather.2.cloned.1.call-done = bf16[8192,6,128]{2,0,1:T(8,128)(2,1)} async-done(((bf16[128,6,128]{2,0,1:T(8,128)(2,1)}), bf16[8192,6,128]{2,0,1:T(8,128)(2,1)}) %all-gather.2.cloned.1.call-update) | async-done | bytes 12582928 | tf_op jit(solution)/shard_map/all_gather | solution.py:12
  262.3 10.1 %fusion.38 = (bf16[8192,3,128]{2,0,1:T(8,128)(2,1)}, bf16[8192,3,128]{2,0,1:T(8,128)(2,1)}) fusion(bf16[8192,6,128]{2,0,1:T(8,128)(2,1)} %all-gather.2.cloned.1.call-done), kind=kLoop, calls=%fused_computation.51 | loop fusion | bytes 25165824 | tf_op jit(solution)/shard_map/slice | solution.py:14
  272.4 19.6 %while.14 = (s32[]{:T(128)}, f32[3,128]{1,0:T(4,128)S(1)}, f32[3,128]{1,0:T(4,128)S(1)}, f32[128,3,128]{0,2,1:T(8,128)S(1)}, pred[4,2048]{1,0:T(4,128)(4,1)S(1)}...) while((s32[]{:T(128)}, f32[3,128]{1,0:T(4,128)S(1)}, ...), condition=%wide.region_5.6_spmd, body=%wide.region_2.5_spmd.sunk | while | flops 408257664 | bytes 13106273 | solution.py:47
  272.4 2.0 bitcast_reduce_fusion.2
  274.4 2.4 fusion.54
  276.8 0.4 fusion.53
  277.3 2.0 bitcast_reduce_fusion.2
  279.4 2.4 fusion.54
  281.7 0.4 fusion.53
  282.2 2.0 bitcast_reduce_fusion.2
  284.3 2.4 fusion.54
  286.6 0.4 fusion.53
  287.1 2.0 bitcast_reduce_fusion.2
  289.2 2.4 fusion.54
  291.5 0.4 fusion.53
  292.0 0.1 copy.62
  292.2 0.1 reshape.75
  292.3 14.2 %all_to_all.96 = bf16[8,16,384]{2,1,0:T(8,128)(2,1)S(1)} all-to-all(bf16[8,16,384]{2,1,0:T(8,128)(2,1)S(1)} %multiply_convert_fusion), channel_id=1, replica_groups=mesh['patch'=64,'uly'=8] {'uly'}, dimensions={0} | all-to-all | bytes 196608 | tf_op jit(solution)/shard_map/all_to_all | solution.py:91
  306.5 0.7 copy.73
  (24 shorter events, 0.5 us)
Async XLA Ops:
  6.5 78.5 %copy-start = (f32[50,3072]{1,0:T(8,128)S(1)}, f32[50,3072]{1,0:T(8,128)}, u32[]{:S(2)}) copy-start(f32[50,3072]{1,0:T(8,128)} %param.14) | copy-start | bytes 1843204
  6.5 60.7 %copy-start.1 = (bf16[16,3072]{1,0:T(8,128)(2,1)S(1)}, bf16[16,3072]{1,0:T(8,128)(2,1)}, u32[]{:S(2)}) copy-start(bf16[16,3072]{1,0:T(8,128)(2,1)} %param.11) | copy-start | bytes 294916
  8.1 23.8 %all-to-all-start.3 = ((bf16[16,8,384]{2,0,1:T(8,128)(2,1)}), bf16[16,8,384]{2,0,1:T(8,128)(2,1)S(1)}, u32[]{:S(2)}, u32[]{:S(2)}) async-start(bf16[16,8,384]{2,0,1:T(8,128)(2,1)} %bitcast.72), calls=%async_computation.3 | async-start | bytes 196608 | tf_op jit(solution)/shard_map/all_to_all | solution.py:76
  31.9 14.8 %all-to-all-start.4 = ((bf16[16,8,384]{2,0,1:T(8,128)(2,1)}), bf16[16,8,384]{2,0,1:T(8,128)(2,1)S(1)}, u32[]{:S(2)}, u32[]{:S(2)}) async-start(bf16[16,8,384]{2,0,1:T(8,128)(2,1)} %bitcast.71), calls=%async_computation.4 | async-start | bytes 196608 | tf_op jit(solution)/shard_map/all_to_all | solution.py:77
  35.5 226.8 %all-gather.2.cloned.1.call-start = ((), (), s32[]{:S(2)}) async-start(), calls=%async_computation.6 | async-start | bytes 12779520 | tf_op jit(solution)/shard_map/all_gather | solution.py:12
  49.2 14.6 %all-to-all-start = ((bf16[16,8,384]{2,0,1:T(8,128)(2,1)}), bf16[16,8,384]{2,0,1:T(8,128)(2,1)S(1)}, u32[]{:S(2)}, u32[]{:S(2)}) async-start(bf16[16,8,384]{2,0,1:T(8,128)(2,1)} %bitcast.75), calls=%async_computation | async-start | bytes 196608 | tf_op jit(solution)/shard_map/all_to_all | solution.py:57
  63.8 17.8 %all-to-all-start.1 = ((bf16[16,8,384]{2,0,1:T(8,128)(2,1)}), bf16[16,8,384]{2,0,1:T(8,128)(2,1)S(1)}, u32[]{:S(2)}, u32[]{:S(2)}) async-start(bf16[16,8,384]{2,0,1:T(8,128)(2,1)} %bitcast.74), calls=%async_computation.1 | async-start | bytes 196608 | tf_op jit(solution)/shard_map/all_to_all | solution.py:58
  81.6 14.6 %all-to-all-start.2 = ((bf16[16,8,384]{2,0,1:T(8,128)(2,1)}), bf16[16,8,384]{2,0,1:T(8,128)(2,1)S(1)}, u32[]{:S(2)}, u32[]{:S(2)}) async-start(bf16[16,8,384]{2,0,1:T(8,128)(2,1)} %bitcast.73), calls=%async_computation.2 | async-start | bytes 196608 | tf_op jit(solution)/shard_map/all_to_all | solution.py:59
Sparse Core Ops, SparseCore 0:
  47.7 214.5 all-gather.1
where the time goes:
time: 315 us; the launch traced here: 314 us
  waiting for transfers between devices  220 us (70%)
  starting transfers between devices  26.4 us (8%)
  local copies, waits for them, and re-layouts  19.1 us (6%)
  matrix products  18.3 us (6%)
  blocking collectives  14.2 us (5%)
  between operations  14.2 us (5%)
    all_gather x1, waiting for transfers between devices, sent_together(): result, at, outs = (lax.all_gather(both, axis, axis=dim, tiled=True), 0, [])  165 us
    all_to_all x1, blocking collectives, body(): return lax.all_to_all(gated, 'uly', split_axis=0, concat_axis=1, tiled=True)  14.2 us
    all_to_all x1, waiting for transfers between devices, body(): lax.all_to_all(keys_new, 'uly', split_axis=1, concat_axis=0, tiled=True)  13.1 us
    all_to_all x1, starting transfers between devices, body(): lax.all_to_all(keys_old, 'uly', split_axis=1, concat_axis=0, tiled=True)  12.5 us
    all_to_all x1, waiting for transfers between devices, body(): lax.all_to_all(values_old, 'uly', split_axis=1, concat_axis=0, tiled=True)  11.1 us
    all_to_all x1, waiting for transfers between devices, body(): lax.all_to_all(values_new, 'uly', split_axis=1, concat_axis=0, tiled=True)  10.6 us
    slice x1, local copies, waits for them, and re-layouts, sent_together(): outs.append(lax.slice_in_dim(result, at, at + a.shape[along], axis=along))  10.1 us
    all_to_all x1, waiting for transfers between devices, body(): lax.all_to_all(keys_old, 'uly', split_axis=1, concat_axis=0, tiled=True)  9.72 us
  transfers between devices with their start and end apart: 6, of which 6 were waited for; matrix products, arithmetic and copies ran while one was open for 2% of the time, Pallas kernels for 0%

commit v1 on v0

--- a/solution.py
+++ b/solution.py
@@ -5,6 +5,12 @@
 
 HEADS = 24
 HEAD_DIM = 128
+
+
+def exchange_blocks(x, mesh_axis, split, join):
+    pieces = jnp.split(x, lax.axis_size(mesh_axis), axis=split)
+    arrived = lax.all_to_all(jnp.stack(pieces), mesh_axis, 0, 0)
+    return jnp.concatenate(arrived, axis=join)
 
 
 def sent_together(arrays, axis, dim, along):
@@ -74,7 +80,7 @@
     carry = (run_max, run_total, accumulated)
     stale = (
         lax.all_to_all(keys_old, "uly", split_axis=1, concat_axis=0, tiled=True),
-        lax.all_to_all(values_old, "uly", split_axis=1, concat_axis=0, tiled=True),
+        exchange_blocks(values_old, "uly", 1, 0),
     )
     stale_keys = stale[0].reshape(-1, heads_here, HEAD_DIM)
     stale_values = stale[1].reshape(-1, heads_here, HEAD_DIM)

time: 315 us -> 322 us (1.022)
  local copies, waits for them, and re-layouts: 19.1 us -> 28.1 us
  waiting for transfers between devices: 220 us -> 212 us
  starting transfers between devices: 26.4 us -> 32 us
    unnamed x4 -> x11, local copies, waits for them, and re-layouts: 0.01 us -> 9.16 us
    all_to_all x1, waiting for transfers between devices: 9.72 us -> 0.8 us  [body(): lax.all_to_all(keys_old, 'uly', split_axis=1, concat_axis=0, tiled=True)]
    all_to_all x1, starting transfers between devices: 3.6 us -> 9.11 us  [exchange_blocks(): arrived = lax.all_to_all(jnp.stack(pieces), mesh_axis, 0, 0)]
  transfers between devices with their start and end apart: 6 -> 6, of which waited for: 6 -> 6; matrix products, arithmetic and copies ran while one was open for 2% -> 5% of each run, Pallas kernels for 0% -> 0%
where the time goes in v1:
time: 322 us; the launch traced here: 321 us
  waiting for transfers between devices  212 us (66%)
  starting transfers between devices  32 us (10%)
  local copies, waits for them, and re-layouts  28.1 us (9%)
  matrix products  18.3 us (6%)
  blocking collectives  14.2 us (4%)
  between operations  14.2 us (4%)
    all_gather x1, waiting for transfers between devices, sent_together(): result, at, outs = (lax.all_gather(both, axis, axis=dim, tiled=True), 0, [])  168 us
    all_to_all x1, blocking collectives, body(): return lax.all_to_all(gated, 'uly', split_axis=0, concat_axis=1, tiled=True)  14.2 us
    all_to_all x1, starting transfers between devices, body(): lax.all_to_all(keys_old, 'uly', split_axis=1, concat_axis=0, tiled=True)  12.5 us
    all_to_all x1, waiting for transfers between devices, body(): lax.all_to_all(keys_new, 'uly', split_axis=1, concat_axis=0, tiled=True)  12 us
    all_to_all x1, waiting for transfers between devices, exchange_blocks(): arrived = lax.all_to_all(jnp.stack(pieces), mesh_axis, 0, 0)  11.1 us
    all_to_all x1, waiting for transfers between devices, body(): lax.all_to_all(values_new, 'uly', split_axis=1, concat_axis=0, tiled=True)  10.6 us
    slice x1, local copies, waits for them, and re-layouts, sent_together(): outs.append(lax.slice_in_dim(result, at, at + a.shape[along], axis=along))  10.1 us
    all_to_all x1, waiting for transfers between devices, body(): lax.all_to_all(queries, 'uly', split_axis=1, concat_axis=0, tiled=True)  9.56 us
  transfers between devices with their start and end apart: 6, of which 6 were waited for; matrix products, arithmetic and copies ran while one was open for 5% of the time, Pallas kernels for 0%

profile of v1, /device:TPU:8, one launch (start us, length us, event | category | flops | bytes accessed | tf_op | source)
XLA Modules:
  0.0 320.9 jit_solution(7305848134880846)
XLA Ops:
  6.5 0.0 copy-start
  6.5 0.0 copy-start.1
  6.5 1.6 copy.81
  8.1 12.5 %all-to-all-start.3 = ((bf16[16,8,384]{2,0,1:T(8,128)(2,1)}), bf16[16,8,384]{2,0,1:T(8,128)(2,1)S(1)}, u32[]{:S(2)}, u32[]{:S(2)}) async-start(bf16[16,8,384]{2,0,1:T(8,128)(2,1)} %bitcast.83), calls=%async_computation.3 | async-start | bytes 196608 | tf_op jit(solution)/shard_map/all_to_all | solution.py:82
  20.7 1.3 constant_dynamic-update-slice_fusion.7
  22.0 1.3 constant_dynamic-update-slice_fusion.6
  23.3 1.3 constant_dynamic-update-slice_fusion.5
  24.6 1.3 constant_dynamic-update-slice_fusion.4
  25.9 1.3 constant_dynamic-update-slice_fusion.3
  27.2 1.3 constant_dynamic-update-slice_fusion.2
  28.5 1.3 constant_dynamic-update-slice_fusion.1
  29.8 1.3 constant_dynamic-update-slice_fusion
  31.1 0.8 all-to-all-done.3
  31.9 9.1 %all-to-all-start.4 = ((bf16[8,16,384]{2,1,0:T(8,128)(2,1)}), bf16[8,16,384]{2,1,0:T(8,128)(2,1)S(1)}, u32[]{:S(2)}, u32[]{:S(2)}) async-start(bf16[8,16,384]{2,1,0:T(8,128)(2,1)} %constant_dynamic-update-slice_fusion), calls=%async_computation.4 | async-start | bytes 196608 | tf_op jit(solution)/shard_map/all_to_all | solution.py:12
  41.0 0.0 all-gather.2.cloned.1.call-start
  41.1 11.1 %all-to-all-done.4 = bf16[8,16,384]{2,1,0:T(8,128)(2,1)S(1)} async-done(((bf16[8,16,384]{2,1,0:T(8,128)(2,1)}), bf16[8,16,384]{2,1,0:T(8,128)(2,1)S(1)}, u32[]{:S(2)}, u32[]{:S(2)}) %all-to-all-start.4) | async-done | bytes 98336 | tf_op jit(solution)/shard_map/all_to_all | solution.py:12
  52.2 0.1 pad_maximum_fusion
  52.4 0.7 copy.55
  53.1 0.0 all-gather.2.cloned.1.call-update
  53.1 1.5 copy.84
  54.7 3.4 %all-to-all-start = ((bf16[16,8,384]{2,0,1:T(8,128)(2,1)}), bf16[16,8,384]{2,0,1:T(8,128)(2,1)S(1)}, u32[]{:S(2)}, u32[]{:S(2)}) async-start(bf16[16,8,384]{2,0,1:T(8,128)(2,1)} %bitcast.86), calls=%async_computation | async-start | bytes 196608 | tf_op jit(solution)/shard_map/all_to_all | solution.py:63
  58.0 1.5 copy.83
  59.6 9.6 %all-to-all-done = bf16[16,8,384]{2,0,1:T(8,128)(2,1)S(1)} async-done(((bf16[16,8,384]{2,0,1:T(8,128)(2,1)}), bf16[16,8,384]{2,0,1:T(8,128)(2,1)S(1)}, u32[]{:S(2)}, u32[]{:S(2)}) %all-to-all-start) | async-done | bytes 98336 | tf_op jit(solution)/shard_map/all_to_all | solution.py:63
  69.1 3.4 %all-to-all-start.1 = ((bf16[16,8,384]{2,0,1:T(8,128)(2,1)}), bf16[16,8,384]{2,0,1:T(8,128)(2,1)S(1)}, u32[]{:S(2)}, u32[]{:S(2)}) async-start(bf16[16,8,384]{2,0,1:T(8,128)(2,1)} %bitcast.85), calls=%async_computation.1 | async-start | bytes 196608 | tf_op jit(solution)/shard_map/all_to_all | solution.py:64
  72.5 0.0 copy-done.1
  72.5 0.7 copy.82
  73.8 12.0 %all-to-all-done.1 = bf16[16,8,384]{2,0,1:T(8,128)(2,1)S(1)} async-done(((bf16[16,8,384]{2,0,1:T(8,128)(2,1)}), bf16[16,8,384]{2,0,1:T(8,128)(2,1)S(1)}, u32[]{:S(2)}, u32[]{:S(2)}) %all-to-all-start.1) | async-done | bytes 98336 | tf_op jit(solution)/shard_map/all_to_all | solution.py:64
  85.8 3.6 %all-to-all-start.2 = ((bf16[16,8,384]{2,0,1:T(8,128)(2,1)}), bf16[16,8,384]{2,0,1:T(8,128)(2,1)S(1)}, u32[]{:S(2)}, u32[]{:S(2)}) async-start(bf16[16,8,384]{2,0,1:T(8,128)(2,1)} %bitcast.84), calls=%async_computation.2 | async-start | bytes 196608 | tf_op jit(solution)/shard_map/all_to_all | solution.py:65
  89.4 0.0 copy-done
  89.4 0.3 fusion.33
  89.8 0.1 dynamic_slice.14
  89.8 0.1 fusion.30
  90.0 10.6 %all-to-all-done.2 = bf16[16,8,384]{2,0,1:T(8,128)(2,1)S(1)} async-done(((bf16[16,8,384]{2,0,1:T(8,128)(2,1)}), bf16[16,8,384]{2,0,1:T(8,128)(2,1)S(1)}, u32[]{:S(2)}, u32[]{:S(2)}) %all-to-all-start.2) | async-done | bytes 98336 | tf_op jit(solution)/shard_map/all_to_all | solution.py:65
  100.6 0.2 fusion.39
  100.8 0.2 convolution_bitcast_fusion
  101.1 0.1 copy.56
  101.2 0.1 fusion.24
  101.3 167.9 %all-gather.2.cloned.1.call-done = bf16[8192,6,128]{2,0,1:T(8,128)(2,1)} async-done(((bf16[128,6,128]{2,0,1:T(8,128)(2,1)}), bf16[8192,6,128]{2,0,1:T(8,128)(2,1)}) %all-gather.2.cloned.1.call-update) | async-done | bytes 12582928 | tf_op jit(solution)/shard_map/all_gather | solution.py:18
  269.2 10.1 %fusion.38 = (bf16[8192,3,128]{2,0,1:T(8,128)(2,1)}, bf16[8192,3,128]{2,0,1:T(8,128)(2,1)}) fusion(bf16[8192,6,128]{2,0,1:T(8,128)(2,1)} %all-gather.2.cloned.1.call-done), kind=kLoop, calls=%fused_computation.58 | loop fusion | bytes 25165824 | tf_op jit(solution)/shard_map/slice | solution.py:20
  279.3 19.6 %while.14 = (s32[]{:T(128)}, f32[3,128]{1,0:T(4,128)S(1)}, f32[3,128]{1,0:T(4,128)S(1)}, f32[128,3,128]{0,2,1:T(8,128)S(1)}, pred[4,2048]{1,0:T(4,128)(4,1)S(1)}...) while((s32[]{:T(128)}, f32[3,128]{1,0:T(4,128)S(1)}, ...), condition=%wide.region_5.6_spmd, body=%wide.region_2.5_spmd.sunk | while | flops 408257664 | bytes 13106273 | solution.py:53
  279.3 2.0 bitcast_reduce_fusion.2
  281.3 2.4 fusion.54
  283.7 0.4 fusion.53
  284.2 2.0 bitcast_reduce_fusion.2
  286.2 2.4 fusion.54
  288.6 0.4 fusion.53
  289.1 2.0 bitcast_reduce_fusion.2
  291.2 2.4 fusion.54
  293.5 0.4 fusion.53
  294.0 2.0 bitcast_reduce_fusion.2
  296.1 2.4 fusion.54
  298.4 0.4 fusion.53
  298.9 0.1 copy.60
  299.1 0.1 reshape.67
  299.2 14.2 %all_to_all.85 = bf16[8,16,384]{2,1,0:T(8,128)(2,1)S(1)} all-to-all(bf16[8,16,384]{2,1,0:T(8,128)(2,1)S(1)} %multiply_convert_fusion), channel_id=1, replica_groups=mesh['patch'=64,'uly'=8] {'uly'}, dimensions={0} | all-to-all | bytes 196608 | tf_op jit(solution)/shard_map/all_to_all | solution.py:97
  313.4 0.7 copy.70
  (24 shorter events, 0.5 us)
Async XLA Ops:
  6.5 82.9 %copy-start = (f32[50,3072]{1,0:T(8,128)S(1)}, f32[50,3072]{1,0:T(8,128)}, u32[]{:S(2)}) copy-start(f32[50,3072]{1,0:T(8,128)} %param.14) | copy-start | bytes 1843204
  6.5 66.0 %copy-start.1 = (bf16[16,3072]{1,0:T(8,128)(2,1)S(1)}, bf16[16,3072]{1,0:T(8,128)(2,1)}, u32[]{:S(2)}) copy-start(bf16[16,3072]{1,0:T(8,128)(2,1)} %param.11) | copy-start | bytes 294916
  8.1 23.8 %all-to-all-start.3 = ((bf16[16,8,384]{2,0,1:T(8,128)(2,1)}), bf16[16,8,384]{2,0,1:T(8,128)(2,1)S(1)}, u32[]{:S(2)}, u32[]{:S(2)}) async-start(bf16[16,8,384]{2,0,1:T(8,128)(2,1)} %bitcast.83), calls=%async_computation.3 | async-start | bytes 196608 | tf_op jit(solution)/shard_map/all_to_all | solution.py:82
  31.9 20.3 %all-to-all-start.4 = ((bf16[8,16,384]{2,1,0:T(8,128)(2,1)}), bf16[8,16,384]{2,1,0:T(8,128)(2,1)S(1)}, u32[]{:S(2)}, u32[]{:S(2)}) async-start(bf16[8,16,384]{2,1,0:T(8,128)(2,1)} %constant_dynamic-update-slice_fusion), calls=%async_computation.4 | async-start | bytes 196608 | tf_op jit(solution)/shard_map/all_to_all | solution.py:12
  41.0 228.1 %all-gather.2.cloned.1.call-start = ((), (), s32[]{:S(2)}) async-start(), calls=%async_computation.6 | async-start | bytes 12779520 | tf_op jit(solution)/shard_map/all_gather | solution.py:18
  54.7 14.5 %all-to-all-start = ((bf16[16,8,384]{2,0,1:T(8,128)(2,1)}), bf16[16,8,384]{2,0,1:T(8,128)(2,1)S(1)}, u32[]{:S(2)}, u32[]{:S(2)}) async-start(bf16[16,8,384]{2,0,1:T(8,128)(2,1)} %bitcast.86), calls=%async_computation | async-start | bytes 196608 | tf_op jit(solution)/shard_map/all_to_all | solution.py:63
  69.1 16.7 %all-to-all-start.1 = ((bf16[16,8,384]{2,0,1:T(8,128)(2,1)}), bf16[16,8,384]{2,0,1:T(8,128)(2,1)S(1)}, u32[]{:S(2)}, u32[]{:S(2)}) async-start(bf16[16,8,384]{2,0,1:T(8,128)(2,1)} %bitcast.85), calls=%async_computation.1 | async-start | bytes 196608 | tf_op jit(solution)/shard_map/all_to_all | solution.py:64
  85.8 14.8 %all-to-all-start.2 = ((bf16[16,8,384]{2,0,1:T(8,128)(2,1)}), bf16[16,8,384]{2,0,1:T(8,128)(2,1)S(1)}, u32[]{:S(2)}, u32[]{:S(2)}) async-start(bf16[16,8,384]{2,0,1:T(8,128)(2,1)} %bitcast.84), calls=%async_computation.2 | async-start | bytes 196608 | tf_op jit(solution)/shard_map/all_to_all | solution.py:65
Sparse Core Ops, SparseCore 0:
  53.2 215.8 all-gather.1
